TPU v7x, 256 devices: a whole 4x4x8 slice. The times are simulated.
256 devices in a mesh: case: 4 (over z_lo), span: 16 (over y, x), vert: 4 (over z_hi, core).
Axes of the slice: x: 4, y: 4, z: 8 (z_hi: 2, z_lo: 4; z = z_hi * 4 + z_lo), core: 2. Of those that a mesh axis runs over, the one named last changes fastest.
Arguments:
- state: float32 [8, 4, 128, 32, 512], P('case', None, 'span', 'vert'), may hold values from -3 to 4.5
- turbine_x: int32 [8, 6], P('case'), may hold values from 128 to 511
- turbine_y: int32 [8, 6], P('case'), may hold values from 0 to 127
- yaw_index: int32 [8], P('case'), may hold values from 0 to 7
Outputs:
- final_state: float32 [8, 4, 128, 32, 512], P('case', None, 'span', 'vert')
All inputs are finite; a program needn't handle non-finite values.
Results may differ from a plain program's by a relative error of at most 0.0003.
Values sent between devices are 32-bit elements; how exact they have to be, the bound alone decides.
A program may use at most 64 MiB of HBM per device.

v0:
```python
import functools
import math

import jax
import jax.numpy as jnp
from jax import lax
from jax.experimental import pallas as pl
from jax.experimental.pallas import tpu as pltpu
from jax.sharding import PartitionSpec as P

STEPS = 3
DISK = 8
VISC = 0.04
THRUST = 0.75
TIME_STEP = 0.1
YAW_STEP = 0.15
MESH = pl.DeviceIdType.MESH

OWN = slice(2, 6)


def roll_s(v, shift):
    return pltpu.roll(v, shift % 8, 0)


def kernel(
    state_ref, tx_ref, ty_ref, yaw_ref, out_ref,
    stage, q, mid, send_z, recv_z, recv_c, fringe, weight, angle_cos, angle_sin, ramp_ref,
    load_sem, hs, hr, fs, fr,
):
    case, span, vert = lax.axis_index("case"), lax.axis_index("span"), lax.axis_index("vert")
    n_case, n_span, n_vert = lax.axis_size("case"), lax.axis_size("span"), lax.axis_size("vert")
    left, right = lax.rem(span + n_span - 1, n_span), lax.rem(span + 1, n_span)
    below, above = lax.rem(vert + n_vert - 1, n_vert), lax.rem(vert + 1, n_vert)
    has_below, has_above = vert > 0, vert < n_vert - 1
    total_y, half_z = 8 * n_span, 4 * n_vert

    loads = [
        pltpu.make_async_copy(state_ref.at[u], stage.at[u], load_sem.at[u]) for u in (0, 1)
    ]
    for copy in loads:
        copy.start()

    barrier = pltpu.get_barrier_semaphore()
    partners = [
        {"span": s, "vert": v} for s in (left, span, right) for v in (below, vert, above)
    ]
    partners.pop(4)
    partners += [
        {"case": lax.rem(case + 1, n_case)},
        {"case": lax.rem(case + n_case - 1, n_case)},
    ]
    for partner in partners:
        pl.semaphore_signal(barrier, inc=1, device_id=partner, device_id_type=MESH)

    sub = lax.broadcasted_iota(jnp.int32, (8, 128), 0)
    lane = lax.broadcasted_iota(jnp.int32, (8, 128), 1)
    low_half = (sub & 1) == 0
    first_lane, last_lane = lane == 0, lane == 127
    along_x = (sub >> 1) * 128 + lane

    wave = jnp.cos((math.pi / 128.0) * (along_x + 1).astype(jnp.float32))
    ramp_ref[...] = jnp.where(sub < 2, 0.5 * (1.0 - wave), 0.0)
    zeros = jnp.zeros((8, 128), jnp.float32)
    half = jnp.where(low_half, 0, 4)
    for u in (0, 1):
        yaw = jnp.full((8, 128), yaw_ref[u], jnp.int32).astype(jnp.float32)
        angle = (yaw - 3.5) * YAW_STEP
        angle_cos[u] = jnp.cos(angle)
        angle_sin[u] = jnp.sin(angle)

        @pl.loop(1, 11)
        def _(row):
            y = span * 8 + row - 2
            total = zeros
            for k in range(tx_ref.shape[1]):
                offset = jnp.full((8, 128), y - ty_ref[u, k], jnp.int32) & (total_y - 1)
                hit = (along_x == tx_ref[u, k]) & (offset < DISK)
                total = total + jnp.where(hit, THRUST, 0.0)
            domain = jnp.full((8, 128), 2 * case + u, jnp.int32)
            for kind, z in enumerate((1, 2, 6)):
                height = half + (vert * 8 + z - 2)
                weight[u, kind, row] = jnp.where((height < half_z) & (domain > 0), total, 0.0)

    @pl.when(jnp.logical_not(has_below))
    def _():
        @pl.loop(0, 8)
        def _(y):
            for par in (0, 1):
                for u in (0, 1):
                    for f in range(4):
                        recv_z[par, u, 0, f, y] = zeros
        for par in (0, 1):
            for u in (0, 1):
                for f in range(4):
                    recv_c[par, u, 0, f] = zeros
                    recv_c[par, u, 2, f] = zeros

    @pl.when(jnp.logical_not(has_above))
    def _():
        @pl.loop(0, 8)
        def _(y):
            for par in (0, 1):
                for u in (0, 1):
                    for f in range(4):
                        recv_z[par, u, 1, f, y] = zeros
        for par in (0, 1):
            for u in (0, 1):
                for f in range(4):
                    recv_c[par, u, 1, f] = zeros
                    recv_c[par, u, 3, f] = zeros

    def remote(src, dst, par, u, k, device):
        return pltpu.make_async_remote_copy(
            src_ref=src, dst_ref=dst, send_sem=hs.at[par, u, k], recv_sem=hr.at[par, u, k],
            device_id=device, device_id_type=MESH,
        )

    def halo_copies(par, u):
        own = q.at[par, u]
        return [
            (remote(own.at[:, 9, 5], recv_c.at[par, u, 0], par, u, 4, {"span": right, "vert": above}), has_above, has_below),
            (remote(own.at[:, 9, 2], recv_c.at[par, u, 1], par, u, 5, {"span": right, "vert": below}), has_below, has_above),
            (remote(own.at[:, 2, 5], recv_c.at[par, u, 2], par, u, 6, {"span": left, "vert": above}), has_above, has_below),
            (remote(own.at[:, 2, 2], recv_c.at[par, u, 3], par, u, 7, {"span": left, "vert": below}), has_below, has_above),
            (remote(send_z.at[par, u, 0], recv_z.at[par, u, 0], par, u, 2, {"vert": above}), has_above, has_below),
            (remote(send_z.at[par, u, 1], recv_z.at[par, u, 1], par, u, 3, {"vert": below}), has_below, has_above),
            (remote(own.at[:, 8:10, OWN], own.at[:, 0:2, OWN], par, u, 0, {"span": right}), None, None),
            (remote(own.at[:, 2:4, OWN], own.at[:, 10:12, OWN], par, u, 1, {"span": left}), None, None),
        ]

    def guarded(condition, action):
        if condition is None:
            action()
        else:
            pl.when(condition)(action)

    def send_halos(par, u):
        @pl.loop(0, 8)
        def _(y):
            for f in range(4):
                z0, z1, z2, z3 = (q[par, u, f, y + 2, z] for z in range(2, 6))
                send_z[par, u, 0, f, y] = jnp.where(low_half, roll_s(z2, -1), z3)
                send_z[par, u, 1, f, y] = jnp.where(low_half, z0, roll_s(z1, 1))

        for copy, sends, _ in halo_copies(par, u):
            guarded(sends, copy.start)

    def receive_halos(par, u):
        for copy, _, receives in halo_copies(par, u):
            guarded(receives, copy.wait_recv)

        @pl.loop(0, 8)
        def _(y):
            for f in range(4):
                z0, z1, z2, z3 = (q[par, u, f, y + 2, z] for z in range(2, 6))
                low, high = recv_z[par, u, 0, f, y], recv_z[par, u, 1, f, y]
                q[par, u, f, y + 2, 0] = jnp.where(low_half, low, roll_s(z2, 1))
                q[par, u, f, y + 2, 1] = jnp.where(low_half, roll_s(low, -1), roll_s(z3, 1))
                q[par, u, f, y + 2, 6] = jnp.where(low_half, roll_s(z0, -1), roll_s(high, 1))
                q[par, u, f, y + 2, 7] = jnp.where(low_half, roll_s(z1, -1), high)

        for f in range(4):
            for row, low, high in ((1, 0, 1), (10, 2, 3)):
                low, high = recv_c[par, u, low, f], recv_c[par, u, high, f]
                q[par, u, f, row, 1] = jnp.where(low_half, roll_s(low, -1), roll_s(q[par, u, f, row, 5], 1))
                q[par, u, f, row, 6] = jnp.where(low_half, roll_s(q[par, u, f, row, 2], -1), roll_s(high, 1))

    def sent_halos(par, u):
        for copy, sends, _ in halo_copies(par, u):
            guarded(sends, copy.wait_send)

    def tendency(ref, u, row, z, cos, sin):
        center, gx, gy, gz, laplace = [], [], [], [], []
        for f in range(4):
            c = ref[f, row, z]
            north, south = ref[f, row + 1, z], ref[f, row - 1, z]
            upper, lower = ref[f, row, z + 1], ref[f, row, z - 1]
            east, west = pltpu.roll(c, 127, 1), pltpu.roll(c, 1, 1)
            east = jnp.where(last_lane, roll_s(east, -2), east)
            west = jnp.where(first_lane, roll_s(west, 2), west)
            center.append(c)
            gx.append(east - west)
            gy.append(north - south)
            gz.append(upper - lower)
            laplace.append(((east + west) + (north + south)) + (upper + lower) - 6.0 * c)
        strain = gx[1] * gx[1] + gy[2] * gy[2] + gz[3] * gz[3] + gy[1] * gy[1] + gz[1] * gz[1]
        viscous = (0.5 * VISC) * jnp.sqrt(4.0 + strain)
        speed = 1.0 + center[1]
        half_u, half_v, half_w = 0.5 * speed, 0.5 * center[2], 0.5 * center[3]
        normal = speed * cos + center[2] * sin
        kind = 0 if z == 1 else 2 if z == 6 else 1
        thrust = normal * jnp.abs(normal) * weight[u, kind, row]
        extra = [
            0.5 * (gx[1] + gy[2] + gz[3]),
            0.5 * gx[0] + thrust * cos,
            0.5 * gy[0] + thrust * sin,
            0.5 * gz[0],
        ]
        rates = [
            viscous * laplace[f] - (half_u * gx[f] + half_v * gy[f] + half_w * gz[f] + extra[f])
            for f in range(4)
        ]
        return center, rates

    def advance(par, nxt, u):
        cos, sin = angle_cos[u], angle_sin[u]
        field = q.at[par, u]

        def first(row, zs):
            for z in zs:
                center, rates = tendency(field, u, row, z, cos, sin)
                for f in range(4):
                    value = center[f] + TIME_STEP * rates[f]
                    if z == 1:
                        value = jnp.where(low_half & edge_low, 0.0, value)
                    if z == 6:
                        value = jnp.where(jnp.logical_not(low_half) & edge_high, 0.0, value)
                    mid[f, row, z] = value

        edge_low = jnp.full((8, 128), vert, jnp.int32) == 0
        edge_high = jnp.full((8, 128), vert, jnp.int32) == n_vert - 1

        @pl.loop(0, 2)
        def _(side):
            first(1 + 9 * side, range(2, 6))

        @pl.loop(2, 10)
        def _(row):
            first(row, range(1, 7))

        sent_halos(par, u)

        @pl.loop(2, 10)
        def _(row):
            for z in range(2, 6):
                center, rates = tendency(mid, u, row, z, cos, sin)
                for f in range(4):
                    q[nxt, u, f, row, z] = 0.5 * (field[f, row, z] + center[f]) + (0.5 * TIME_STEP) * rates[f]

    def blend(nxt, u, s):
        ramp = ramp_ref[...]

        @pl.loop(0, 8)
        def _(y):
            for f in range(4):
                packed = fringe[s, f, y]
                for k in range(4):
                    value = q[nxt, u, f, y + 2, 2 + k]
                    q[nxt, u, f, y + 2, 2 + k] = value + ramp * (roll_s(packed, -2 * k) - value)

    def fringe_copy(s, f):
        return pltpu.make_async_remote_copy(
            src_ref=fringe.at[s, f], dst_ref=fringe.at[s, f], send_sem=fs.at[s, f], recv_sem=fr.at[s, f],
            device_id={"case": lax.rem(case + 1, n_case)}, device_id_type=MESH,
        )

    def pack_fringe(nxt, s):
        for f in range(4):
            @pl.loop(0, 8)
            def _(y):
                parts = [roll_s(q[nxt, 0, f, y + 2, 2 + k], 2 * k) if k else q[nxt, 0, f, y + 2, 2] for k in range(4)]
                fringe[s, f, y] = jnp.where(
                    sub < 4, jnp.where(sub < 2, parts[0], parts[1]), jnp.where(sub < 6, parts[2], parts[3])
                )

            fringe_copy(s, f).start()

    def emit(nxt, u):
        @pl.loop(0, 8)
        def _(y):
            for f in range(4):
                for k in range(4):
                    out_ref[u, f, y, pl.ds(k, 8, stride=4), :] = q[nxt, u, f, y + 2, 2 + k]

    for u in (0, 1):
        loads[u].wait()

        @pl.loop(0, 8)
        def _(y):
            for f in range(4):
                for k in range(4):
                    q[0, u, f, y + 2, 2 + k] = stage[u, f, y, pl.ds(k, 8, stride=4), :]

        if u == 0:
            pl.semaphore_wait(barrier, len(partners))
        send_halos(0, u)

    @pl.loop(0, STEPS)
    def _(s):
        par = lax.rem(s, 2)
        nxt = 1 - par
        more = s < STEPS - 1
        receive_halos(par, 0)
        advance(par, nxt, 0)

        @pl.when(case == 0)
        def _():
            pack_fringe(nxt, s)

        @pl.when((case == 0) & more)
        def _():
            send_halos(nxt, 0)

        receive_halos(par, 1)
        advance(par, nxt, 1)

        @pl.when(case > 0)
        def _():
            for f in range(4):
                fringe_copy(s, f).wait_recv()
                pl.when(case < n_case - 1)(fringe_copy(s, f).start)
            blend(nxt, 0, s)

        @pl.when((case > 0) & more)
        def _():
            send_halos(nxt, 0)

        blend(nxt, 1, s)

        @pl.when(more)
        def _():
            send_halos(nxt, 1)

        @pl.when(case < n_case - 1)
        def _():
            for f in range(4):
                fringe_copy(s, f).wait_send()

    for u in (0, 1):
        emit(STEPS % 2, u)


def body(state, turbine_x, turbine_y, yaw_index):
    slots, fields, rows_y, rows_z, x = state.shape
    tiles = x // 128
    tiled = state.reshape(slots, fields, rows_y, rows_z, tiles, 128).transpose(0, 1, 2, 4, 3, 5)
    tiled = tiled.reshape(slots, fields, rows_y, tiles * rows_z, 128)
    domain = (2, 4, 12, 8, 8, 128)
    out = pl.pallas_call(
        kernel,
        out_shape=jax.ShapeDtypeStruct(tiled.shape, jnp.float32),
        in_specs=[pl.BlockSpec(memory_space=pl.ANY)] + [pl.BlockSpec(memory_space=pltpu.SMEM)] * 3,
        out_specs=pl.BlockSpec(memory_space=pltpu.VMEM),
        scratch_shapes=[
            pltpu.VMEM(tiled.shape, jnp.float32),
            pltpu.VMEM((2,) + domain, jnp.float32),
            pltpu.VMEM(domain[1:], jnp.float32),
            pltpu.VMEM((2, 2, 2, 4, 8, 8, 128), jnp.float32),
            pltpu.VMEM((2, 2, 2, 4, 8, 8, 128), jnp.float32),
            pltpu.VMEM((2, 2, 4, 4, 8, 128), jnp.float32),
            pltpu.VMEM((STEPS, 4, 8, 8, 128), jnp.float32),
            pltpu.VMEM((2, 3, 12, 8, 128), jnp.float32),
            pltpu.VMEM((2, 8, 128), jnp.float32),
            pltpu.VMEM((2, 8, 128), jnp.float32),
            pltpu.VMEM((8, 128), jnp.float32),
            pltpu.SemaphoreType.DMA((2,)),
            pltpu.SemaphoreType.DMA((2, 2, 8)),
            pltpu.SemaphoreType.DMA((2, 2, 8)),
            pltpu.SemaphoreType.DMA((STEPS, 4)),
            pltpu.SemaphoreType.DMA((STEPS, 4)),
        ],
        compiler_params=pltpu.CompilerParams(
            collective_id=0, has_side_effects=True, vmem_limit_bytes=40 << 20
        ),
        name="heun_steps",
    )(tiled, turbine_x, turbine_y, yaw_index)
    out = out.reshape(slots, fields, rows_y, tiles, rows_z, 128).transpose(0, 1, 2, 4, 3, 5)
    return out.reshape(state.shape)


def solution(mesh):
    return jax.shard_map(
        body,
        mesh=mesh,
        in_specs=(
            P("case", None, "span", "vert", None),
            P("case", None),
            P("case", None),
            P("case"),
        ),
        out_specs=P("case", None, "span", "vert", None),
        check_vma=False,
    )
```

profile of v0, /device:TPU:96, one launch (start us, length us, event | category | flops | bytes accessed | tf_op | source)
XLA Modules:
  0.0 68.5 jit_solution(17615558956550959807)
XLA Ops:
  0.0 0.0 copy-start.3
  0.0 0.0 copy-start.1
  0.0 0.7 copy-done.3
  0.7 0.0 copy-done.1
  0.7 0.0 copy-start
  0.7 1.2 %copy-done = f32[2,4,8,8,512]{4,3,2,1,0:T(8,128)S(1)} copy-done((f32[2,4,8,8,512]{4,3,2,1,0:T(8,128)S(1)}, f32[2,4,8,8,512]{4,3,2,1,0:T(8,128)}, u32[]{:S(2)}) %copy-start) | copy-done | bytes 1048600
  1.9 0.0 copy-start.2
  1.9 0.7 copy-done.2
  2.6 65.0 %heun_steps.1 = f32[2,4,8,32,128]{4,3,2,1,0:T(8,128)S(1)} custom-call(f32[2,4,8,32,128]{4,3,2,1,0:T(8,128)S(1)} %bitcast.11, s32[2,6]{1,0:T(2,128)S(1)} %copy-done.1, s32[2,6]{1,0:T(2,128)S(1)} %copy-done.2, s32[2]{0:T(128)S(1)} %copy-done.3), custom_call_target="tpu_custom_call" | custom-call | tf_op jit(solution)/shard_map/heun_steps/pallas_call | solution.py:340
  67.6 1.0 %copy.6 = f32[2,4,8,8,512]{4,3,2,1,0:T(8,128)} copy(f32[2,4,8,8,512]{4,3,2,1,0:T(8,128)S(1)} %bitcast.10) | data formatting | bytes 2097152
Async XLA Ops:
  0.0 0.7 copy-start.3
  0.0 0.7 %copy-start.1 = (s32[2,6]{1,0:T(2,128)S(1)}, s32[2,6]{1,0:T(2,128)}, u32[]{:S(2)}) copy-start(s32[2,6]{1,0:T(2,128)} %tx_ref.1) | copy-start | bytes 148
  0.7 1.2 %copy-start = (f32[2,4,8,8,512]{4,3,2,1,0:T(8,128)S(1)}, f32[2,4,8,8,512]{4,3,2,1,0:T(8,128)}, u32[]{:S(2)}) copy-start(f32[2,4,8,8,512]{4,3,2,1,0:T(8,128)} %param.4) | copy-start | bytes 3145732
  1.9 0.7 copy-start.2
where the time goes:
time: 69 us; the launch traced here: 68.5 us
  Pallas kernels  65 us (94%)
  local copies, waits for them, and re-layouts  3.57 us (5%)
    pallas_call x1, Pallas kernels, body(): pl.pallas_call(kernel, out_shape=jax.ShapeDtypeStruct(tiled.shape, jnp.fl...  65 us
    unnamed x9, local copies, waits for them, and re-layouts  3.57 us

commit v1 on v0

v1 whole, which is shorter than its diff:
```python
import functools
import math

import jax
import jax.numpy as jnp
from jax import lax
from jax.experimental import pallas as pl
from jax.experimental.pallas import tpu as pltpu
from jax.sharding import PartitionSpec as P

STEPS = 3
DISK = 8
VISC = 0.04
THRUST = 0.75
TIME_STEP = 0.1
YAW_STEP = 0.15
MESH = pl.DeviceIdType.MESH

OWN = slice(2, 6)


def roll_s(v, shift):
    return pltpu.roll(v, shift % 8, 0)


def kernel(
    state_ref, tx_hbm, ty_hbm, yaw_hbm, out_ref,
    stage, q, mid, send_z, recv_z, recv_c, fringe, weight, angle_cos, angle_sin, ramp_ref, tx_ref, ty_ref, yaw_ref,
    load_sem, hs, hr, fs, fr,
):
    case, span, vert = lax.axis_index("case"), lax.axis_index("span"), lax.axis_index("vert")
    n_case, n_span, n_vert = lax.axis_size("case"), lax.axis_size("span"), lax.axis_size("vert")
    left, right = lax.rem(span + n_span - 1, n_span), lax.rem(span + 1, n_span)
    below, above = lax.rem(vert + n_vert - 1, n_vert), lax.rem(vert + 1, n_vert)
    has_below, has_above = vert > 0, vert < n_vert - 1
    total_y, half_z = 8 * n_span, 4 * n_vert

    loads = [
        pltpu.make_async_copy(state_ref.at[u], stage.at[u], load_sem.at[u]) for u in (0, 1)
    ]
    loads += [
        pltpu.make_async_copy(src, dst, load_sem.at[2 + i])
        for i, (src, dst) in enumerate(((tx_hbm, tx_ref), (ty_hbm, ty_ref), (yaw_hbm, yaw_ref)))
    ]
    for copy in loads:
        copy.start()

    barrier = pltpu.get_barrier_semaphore()
    partners = [
        {"span": s, "vert": v} for s in (left, span, right) for v in (below, vert, above)
    ]
    partners.pop(4)
    partners += [
        {"case": lax.rem(case + k, n_case)} for k in range(1, 4)
    ]
    for partner in partners:
        pl.semaphore_signal(barrier, inc=1, device_id=partner, device_id_type=MESH)

    sub = lax.broadcasted_iota(jnp.int32, (8, 128), 0)
    lane = lax.broadcasted_iota(jnp.int32, (8, 128), 1)
    low_half = (sub & 1) == 0
    first_lane, last_lane = lane == 0, lane == 127
    along_x = (sub >> 1) * 128 + lane

    zeros = jnp.zeros((8, 128), jnp.float32)

    def constants():
        for copy in loads[2:]:
            copy.wait()
        wave = jnp.cos((math.pi / 128.0) * (along_x + 1).astype(jnp.float32))
        ramp_ref[...] = jnp.where(sub < 2, 0.5 * (1.0 - wave), 0.0)
        half = jnp.where(low_half, 0, 4)
        for u in (0, 1):
            yaw = jnp.full((8, 128), yaw_ref[u], jnp.int32).astype(jnp.float32)
            angle = (yaw - 3.5) * YAW_STEP
            angle_cos[u] = jnp.cos(angle)
            angle_sin[u] = jnp.sin(angle)

            @pl.loop(1, 11)
            def _(row):
                y = span * 8 + row - 2
                total = zeros
                for k in range(tx_ref.shape[1]):
                    offset = jnp.full((8, 128), y - ty_ref[u, k], jnp.int32) & (total_y - 1)
                    hit = (along_x == tx_ref[u, k]) & (offset < DISK)
                    total = total + jnp.where(hit, THRUST, 0.0)
                domain = jnp.full((8, 128), 2 * case + u, jnp.int32)
                for kind, z in enumerate((1, 2, 6)):
                    height = half + (vert * 8 + z - 2)
                    weight[u, kind, row] = jnp.where((height < half_z) & (domain > 0), total, 0.0)

        @pl.when(jnp.logical_not(has_below))
        def _():
            @pl.loop(0, 4)
            def _(y):
                for par in (0, 1):
                    for u in (0, 1):
                        for f in range(4):
                            recv_z[par, u, 0, 0, f, y] = zeros
                            recv_z[par, u, 0, 1, f, y] = zeros
            for par in (0, 1):
                for u in (0, 1):
                    for f in range(4):
                        recv_c[par, u, 0, f] = zeros
                        recv_c[par, u, 2, f] = zeros

        @pl.when(jnp.logical_not(has_above))
        def _():
            @pl.loop(0, 4)
            def _(y):
                for par in (0, 1):
                    for u in (0, 1):
                        for f in range(4):
                            recv_z[par, u, 1, 0, f, y] = zeros
                            recv_z[par, u, 1, 1, f, y] = zeros
            for par in (0, 1):
                for u in (0, 1):
                    for f in range(4):
                        recv_c[par, u, 1, f] = zeros
                        recv_c[par, u, 3, f] = zeros

    def remote(src, dst, par, u, k, device):
        return pltpu.make_async_remote_copy(
            src_ref=src, dst_ref=dst, send_sem=hs.at[par, u, k], recv_sem=hr.at[par, u, k],
            device_id=device, device_id_type=MESH,
        )

    def halo_copies(par, u, part):
        own = q.at[par, u]
        if part == "corner":
            return [
                (remote(own.at[:, 9, 5], recv_c.at[par, u, 0], par, u, 4, {"span": right, "vert": above}), has_above, has_below),
                (remote(own.at[:, 9, 2], recv_c.at[par, u, 1], par, u, 5, {"span": right, "vert": below}), has_below, has_above),
                (remote(own.at[:, 2, 5], recv_c.at[par, u, 2], par, u, 6, {"span": left, "vert": above}), has_above, has_below),
                (remote(own.at[:, 2, 2], recv_c.at[par, u, 3], par, u, 7, {"span": left, "vert": below}), has_below, has_above),
            ]
        if part == "inner":
            return [
                (remote(send_z.at[par, u, 0, 0], recv_z.at[par, u, 0, 0], par, u, 0, {"vert": above}), has_above, has_below),
                (remote(send_z.at[par, u, 1, 0], recv_z.at[par, u, 1, 0], par, u, 1, {"vert": below}), has_below, has_above),
                (remote(own.at[:, 9, OWN], own.at[:, 1, OWN], par, u, 2, {"span": right}), None, None),
                (remote(own.at[:, 2, OWN], own.at[:, 10, OWN], par, u, 3, {"span": left}), None, None),
            ]
        return [
            (remote(send_z.at[par, u, 0, 1], recv_z.at[par, u, 0, 1], par, u, 8, {"vert": above}), has_above, has_below),
            (remote(send_z.at[par, u, 1, 1], recv_z.at[par, u, 1, 1], par, u, 9, {"vert": below}), has_below, has_above),
            (remote(own.at[:, 8, OWN], own.at[:, 0, OWN], par, u, 10, {"span": right}), None, None),
            (remote(own.at[:, 3, OWN], own.at[:, 11, OWN], par, u, 11, {"span": left}), None, None),
        ]

    def guarded(condition, action):
        if condition is None:
            action()
        else:
            pl.when(condition)(action)

    def send_halos(par, u):
        for copy, sends, _ in halo_copies(par, u, "corner"):
            guarded(sends, copy.start)

        @pl.loop(0, 4)
        def _(y):
            for f in range(4):
                even = [q[par, u, f, 2 * y + 2, z] for z in range(2, 6)]
                odd = [q[par, u, f, 2 * y + 3, z] for z in range(2, 6)]
                send_z[par, u, 0, 0, f, y] = jnp.where(low_half, roll_s(even[3], -1), odd[3])
                send_z[par, u, 0, 1, f, y] = jnp.where(low_half, roll_s(even[2], -1), odd[2])
                send_z[par, u, 1, 0, f, y] = jnp.where(low_half, even[0], roll_s(odd[0], 1))
                send_z[par, u, 1, 1, f, y] = jnp.where(low_half, even[1], roll_s(odd[1], 1))

        for copy, sends, _ in halo_copies(par, u, "inner") + halo_copies(par, u, "outer"):
            guarded(sends, copy.start)

    def merge_z(par, u, layer):
        @pl.loop(0, 4)
        def _(y):
            for f in range(4):
                low, high = recv_z[par, u, 0, layer, f, y], recv_z[par, u, 1, layer, f, y]
                for odd in (0, 1):
                    row = 2 * y + 2 + odd
                    near_low, near_high = q[par, u, f, row, 5 - layer], q[par, u, f, row, 2 + layer]
                    q[par, u, f, row, 1 - layer] = jnp.where(low_half, roll_s(low, -1) if odd else low, roll_s(near_low, 1))
                    q[par, u, f, row, 6 + layer] = jnp.where(low_half, roll_s(near_high, -1), high if odd else roll_s(high, 1))

    def receive_inner(par, u):
        for copy, _, receives in halo_copies(par, u, "inner"):
            guarded(receives, copy.wait_recv)
        merge_z(par, u, 0)

    def receive_outer(par, u):
        for copy, _, receives in halo_copies(par, u, "outer"):
            guarded(receives, copy.wait_recv)
        merge_z(par, u, 1)

    def receive_corners(par, u):
        for copy, _, receives in halo_copies(par, u, "corner"):
            guarded(receives, copy.wait_recv)
        for f in range(4):
            for row, low, high in ((1, 0, 1), (10, 2, 3)):
                low, high = recv_c[par, u, low, f], recv_c[par, u, high, f]
                q[par, u, f, row, 1] = jnp.where(low_half, roll_s(low, -1), roll_s(q[par, u, f, row, 5], 1))
                q[par, u, f, row, 6] = jnp.where(low_half, roll_s(q[par, u, f, row, 2], -1), roll_s(high, 1))

    def sent_halos(par, u):
        for part in ("corner", "inner", "outer"):
            for copy, sends, _ in halo_copies(par, u, part):
                guarded(sends, copy.wait_send)

    def tendency(ref, u, row, z, cos, sin):
        center, gx, gy, gz, laplace = [], [], [], [], []
        for f in range(4):
            c = ref[f, row, z]
            north, south = ref[f, row + 1, z], ref[f, row - 1, z]
            upper, lower = ref[f, row, z + 1], ref[f, row, z - 1]
            east, west = pltpu.roll(c, 127, 1), pltpu.roll(c, 1, 1)
            east = jnp.where(last_lane, roll_s(east, -2), east)
            west = jnp.where(first_lane, roll_s(west, 2), west)
            center.append(c)
            gx.append(east - west)
            gy.append(north - south)
            gz.append(upper - lower)
            laplace.append(((east + west) + (north + south)) + (upper + lower) - 6.0 * c)
        strain = gx[1] * gx[1] + gy[2] * gy[2] + gz[3] * gz[3] + gy[1] * gy[1] + gz[1] * gz[1]
        viscous = (0.5 * VISC) * jnp.sqrt(4.0 + strain)
        speed = 1.0 + center[1]
        half_u, half_v, half_w = 0.5 * speed, 0.5 * center[2], 0.5 * center[3]
        normal = speed * cos + center[2] * sin
        kind = 0 if z == 1 else 2 if z == 6 else 1
        thrust = normal * jnp.abs(normal) * weight[u, kind, row]
        extra = [
            0.5 * (gx[1] + gy[2] + gz[3]),
            0.5 * gx[0] + thrust * cos,
            0.5 * gy[0] + thrust * sin,
            0.5 * gz[0],
        ]
        rates = [
            viscous * laplace[f] - (half_u * gx[f] + half_v * gy[f] + half_w * gz[f] + extra[f])
            for f in range(4)
        ]
        return center, rates

    def advance(par, nxt, u, s):
        cos, sin = angle_cos[u], angle_sin[u]
        field = q.at[par, u]

        def first(row, zs):
            for z in zs:
                center, rates = tendency(field, u, row, z, cos, sin)
                for f in range(4):
                    value = center[f] + TIME_STEP * rates[f]
                    if z == 1:
                        value = jnp.where(low_half & edge_low, 0.0, value)
                    if z == 6:
                        value = jnp.where(jnp.logical_not(low_half) & edge_high, 0.0, value)
                    mid[f, row, z] = value

        edge_low = jnp.full((8, 128), vert, jnp.int32) == 0
        edge_high = jnp.full((8, 128), vert, jnp.int32) == n_vert - 1

        @pl.loop(3, 9, step=3)
        def _(row):
            for r in range(3):
                first(row + r, (3, 4))

        receive_inner(par, u)

        first(2, range(2, 6))
        first(9, range(2, 6))

        @pl.loop(3, 9, step=3)
        def _(row):
            for r in range(3):
                first(row + r, (2, 5))

        receive_outer(par, u)

        first(1, (3, 4))
        first(10, (3, 4))

        @pl.loop(3, 9, step=3)
        def _(row):
            for r in range(3):
                first(row + r, (1, 6))

        def second(row, zs):
            for z in zs:
                center, rates = tendency(mid, u, row, z, cos, sin)
                for f in range(4):
                    q[nxt, u, f, row, z] = 0.5 * (field[f, row, z] + center[f]) + (0.5 * TIME_STEP) * rates[f]

        pl.when(s > 0)(lambda: sent_halos(1 - par, u))

        @pl.loop(3, 9, step=2)
        def _(row):
            second(row, range(2, 6))
            second(row + 1, range(2, 6))

        second(2, (3, 4))
        second(9, (3, 4))

        receive_corners(par, u)

        for row, z in ((1, 2), (1, 5), (10, 2), (10, 5), (2, 1), (2, 6), (9, 1), (9, 6)):
            first(row, (z,))
        for row, z in ((2, 2), (2, 5), (9, 2), (9, 5)):
            second(row, (z,))

    def blend(nxt, u, s):
        ramp = ramp_ref[...]

        @pl.loop(0, 8)
        def _(y):
            for f in range(4):
                packed = fringe[s, f, y]
                for k in range(4):
                    value = q[nxt, u, f, y + 2, 2 + k]
                    q[nxt, u, f, y + 2, 2 + k] = value + ramp * (roll_s(packed, -2 * k) - value)

    def fringe_copy(s, f, k=1):
        return pltpu.make_async_remote_copy(
            src_ref=fringe.at[s, f], dst_ref=fringe.at[s, f], send_sem=fs.at[s, f, k], recv_sem=fr.at[s, f],
            device_id={"case": lax.rem(case + k, n_case)}, device_id_type=MESH,
        )

    def pack_fringe(nxt, s):
        for f in range(4):
            @pl.loop(0, 8)
            def _(y):
                parts = [roll_s(q[nxt, 0, f, y + 2, 2 + k], 2 * k) if k else q[nxt, 0, f, y + 2, 2] for k in range(4)]
                fringe[s, f, y] = jnp.where(
                    sub < 4, jnp.where(sub < 2, parts[0], parts[1]), jnp.where(sub < 6, parts[2], parts[3])
                )

            fringe_copy(s, f, 2).start()
            fringe_copy(s, f, 1).start()

    def emit(nxt, u):
        @pl.loop(0, 8)
        def _(y):
            for f in range(4):
                for k in range(4):
                    out_ref[u, f, y, pl.ds(k, 8, stride=4), :] = q[nxt, u, f, y + 2, 2 + k]

    for u in (0, 1):
        loads[u].wait()

        @pl.loop(0, 8)
        def _(y):
            for f in range(4):
                for k in range(4):
                    q[0, u, f, y + 2, 2 + k] = stage[u, f, y, pl.ds(k, 8, stride=4), :]

        if u == 0:
            pl.semaphore_wait(barrier, len(partners))
        send_halos(0, u)

    constants()

    @pl.loop(0, STEPS)
    def _(s):
        par = lax.rem(s, 2)
        nxt = 1 - par
        more = s < STEPS - 1
        advance(par, nxt, 0, s)

        @pl.when(case == 0)
        def _():
            pack_fringe(nxt, s)

        @pl.when((case == 0) & more)
        def _():
            send_halos(nxt, 0)

        def finish_first():
            for f in range(4):
                fringe_copy(s, f).wait_recv()
                pl.when(case == 2)(fringe_copy(s, f).start)
            blend(nxt, 0, s)

            @pl.when(more)
            def _():
                send_halos(nxt, 0)

        pl.when((case > 0) & (s > 0))(finish_first)

        advance(par, nxt, 1, s)

        pl.when((case > 0) & (s == 0))(finish_first)

        blend(nxt, 1, s)

        @pl.when(more)
        def _():
            send_halos(nxt, 1)

        @pl.when(case == 0)
        def _():
            for f in range(4):
                for k in (1, 2):
                    fringe_copy(s, f, k).wait_send()

        @pl.when(case == 2)
        def _():
            for f in range(4):
                fringe_copy(s, f).wait_send()

    for u in (0, 1):
        emit(STEPS % 2, u)
    for u in (0, 1):
        sent_halos((STEPS - 1) % 2, u)


def body(state, turbine_x, turbine_y, yaw_index):
    slots, fields, rows_y, rows_z, x = state.shape
    tiles = x // 128
    tiled = state.reshape(slots, fields, rows_y, rows_z, tiles, 128).transpose(0, 1, 2, 4, 3, 5)
    tiled = tiled.reshape(slots, fields, rows_y, tiles * rows_z, 128)
    domain = (2, 4, 12, 8, 8, 128)
    out = pl.pallas_call(
        kernel,
        out_shape=jax.ShapeDtypeStruct(tiled.shape, jnp.float32),
        in_specs=[pl.BlockSpec(memory_space=pltpu.HBM)] + [pl.BlockSpec(memory_space=pltpu.HBM)] * 3,
        out_specs=pl.BlockSpec(memory_space=pltpu.VMEM),
        scratch_shapes=[
            pltpu.VMEM(tiled.shape, jnp.float32),
            pltpu.VMEM((2,) + domain, jnp.float32),
            pltpu.VMEM(domain[1:], jnp.float32),
            pltpu.VMEM((2, 2, 2, 2, 4, 4, 8, 128), jnp.float32),
            pltpu.VMEM((2, 2, 2, 2, 4, 4, 8, 128), jnp.float32),
            pltpu.VMEM((2, 2, 4, 4, 8, 128), jnp.float32),
            pltpu.VMEM((STEPS, 4, 8, 8, 128), jnp.float32),
            pltpu.VMEM((2, 3, 12, 8, 128), jnp.float32),
            pltpu.VMEM((2, 8, 128), jnp.float32),
            pltpu.VMEM((2, 8, 128), jnp.float32),
            pltpu.VMEM((8, 128), jnp.float32),
            pltpu.SMEM(turbine_x.shape, jnp.int32),
            pltpu.SMEM(turbine_y.shape, jnp.int32),
            pltpu.SMEM(yaw_index.shape, jnp.int32),
            pltpu.SemaphoreType.DMA((5,)),
            pltpu.SemaphoreType.DMA((2, 2, 12)),
            pltpu.SemaphoreType.DMA((2, 2, 12)),
            pltpu.SemaphoreType.DMA((STEPS, 4, 4)),
            pltpu.SemaphoreType.DMA((STEPS, 4)),
        ],
        compiler_params=pltpu.CompilerParams(
            collective_id=0, has_side_effects=True, vmem_limit_bytes=60 << 20
        ),
        name="heun_steps",
    )(tiled, turbine_x, turbine_y, yaw_index)
    out = out.reshape(slots, fields, rows_y, tiles, rows_z, 128).transpose(0, 1, 2, 4, 3, 5)
    return out.reshape(state.shape)


def solution(mesh):
    return jax.shard_map(
        body,
        mesh=mesh,
        in_specs=(
            P("case", None, "span", "vert", None),
            P("case", None),
            P("case", None),
            P("case"),
        ),
        out_specs=P("case", None, "span", "vert", None),
        check_vma=False,
    )
```

time: 69 us -> 62 us (0.90)
  Pallas kernels: 65 us -> 59.2 us
  local copies, waits for them, and re-layouts: 3.57 us -> 2.26 us
    pallas_call x1, Pallas kernels: 65 us -> 59.2 us  [body(): pl.pallas_call(kernel, out_shape=jax.ShapeDtypeStruct(tiled.shape, jnp.fl...]
    unnamed x9 -> x1, local copies, waits for them, and re-layouts: 3.57 us -> 2.26 us
where the time goes in v1:
time: 62 us; the launch traced here: 61.4 us
  Pallas kernels  59.2 us (95%)
  local copies, waits for them, and re-layouts  2.26 us (4%)
    pallas_call x1, Pallas kernels, body(): pl.pallas_call(kernel, out_shape=jax.ShapeDtypeStruct(tiled.shape, jnp.fl...  59.2 us
    unnamed x1, local copies, waits for them, and re-layouts  2.26 us

profile of v1, /device:TPU:96, one launch (start us, length us, event | category | flops | bytes accessed | tf_op | source)
XLA Modules:
  0.0 61.4 jit_solution(15022968763012915379)
XLA Ops:
  0.0 59.2 %heun_steps.1 = f32[2,4,8,32,128]{4,3,2,1,0:T(8,128)} custom-call(f32[2,4,8,32,128]{4,3,2,1,0:T(8,128)} %bitcast.11, s32[2,6]{1,0:T(2,128)} %tx_hbm.1, s32[2,6]{1,0:T(2,128)} %ty_hbm.1, s32[2]{0:T(128)} %yaw_hbm.1), custom_call_target="tpu_custom_call" | custom-call | tf_op jit(solution)/shard_map/heun_steps/pallas_call | solution.py:419
  59.2 2.3 %copy.6 = f32[2,4,8,8,512]{4,3,2,1,0:T(8,128)} copy(f32[2,4,8,8,512]{4,3,2,1,0:T(8,128)} %bitcast.10) | data formatting | bytes 2097152

commit v2 on v1

--- a/solution.py
+++ b/solution.py
@@ -25,7 +25,7 @@
 
 def kernel(
     state_ref, tx_hbm, ty_hbm, yaw_hbm, out_ref,
-    stage, q, mid, send_z, recv_z, recv_c, fringe, weight, angle_cos, angle_sin, ramp_ref, tx_ref, ty_ref, yaw_ref,
+    stage, q, mid, send_z, recv_z, send_c, recv_c, fringe, weight, angle_cos, angle_sin, ramp_ref, tx_ref, ty_ref, yaw_ref,
     load_sem, hs, hr, fs, fr,
 ):
     case, span, vert = lax.axis_index("case"), lax.axis_index("span"), lax.axis_index("vert")
@@ -100,7 +100,7 @@
                             recv_z[par, u, 0, 1, f, y] = zeros
             for par in (0, 1):
                 for u in (0, 1):
-                    for f in range(4):
+                    for f in range(2):
                         recv_c[par, u, 0, f] = zeros
                         recv_c[par, u, 2, f] = zeros
 
@@ -115,7 +115,7 @@
                             recv_z[par, u, 1, 1, f, y] = zeros
             for par in (0, 1):
                 for u in (0, 1):
-                    for f in range(4):
+                    for f in range(2):
                         recv_c[par, u, 1, f] = zeros
                         recv_c[par, u, 3, f] = zeros
 
@@ -129,10 +129,10 @@
         own = q.at[par, u]
         if part == "corner":
             return [
-                (remote(own.at[:, 9, 5], recv_c.at[par, u, 0], par, u, 4, {"span": right, "vert": above}), has_above, has_below),
-                (remote(own.at[:, 9, 2], recv_c.at[par, u, 1], par, u, 5, {"span": right, "vert": below}), has_below, has_above),
-                (remote(own.at[:, 2, 5], recv_c.at[par, u, 2], par, u, 6, {"span": left, "vert": above}), has_above, has_below),
-                (remote(own.at[:, 2, 2], recv_c.at[par, u, 3], par, u, 7, {"span": left, "vert": below}), has_below, has_above),
+                (remote(send_c.at[par, u, 0], recv_c.at[par, u, 0], par, u, 4, {"span": right, "vert": above}), has_above, has_below),
+                (remote(send_c.at[par, u, 1], recv_c.at[par, u, 1], par, u, 5, {"span": right, "vert": below}), has_below, has_above),
+                (remote(send_c.at[par, u, 2], recv_c.at[par, u, 2], par, u, 6, {"span": left, "vert": above}), has_above, has_below),
+                (remote(send_c.at[par, u, 3], recv_c.at[par, u, 3], par, u, 7, {"span": left, "vert": below}), has_below, has_above),
             ]
         if part == "inner":
             return [
@@ -155,6 +155,11 @@
             pl.when(condition)(action)
 
     def send_halos(par, u):
+        for k, (row, z) in enumerate(((9, 5), (9, 2), (2, 5), (2, 2))):
+            for f in (0, 2):
+                even, odd = q[par, u, f, row, z], q[par, u, f + 1, row, z]
+                pair = (roll_s(even, -1), odd) if z == 5 else (even, roll_s(odd, 1))
+                send_c[par, u, k, f // 2] = jnp.where(low_half, *pair)
         for copy, sends, _ in halo_copies(par, u, "corner"):
             guarded(sends, copy.start)
 
@@ -197,9 +202,13 @@
             guarded(receives, copy.wait_recv)
         for f in range(4):
             for row, low, high in ((1, 0, 1), (10, 2, 3)):
-                low, high = recv_c[par, u, low, f], recv_c[par, u, high, f]
-                q[par, u, f, row, 1] = jnp.where(low_half, roll_s(low, -1), roll_s(q[par, u, f, row, 5], 1))
-                q[par, u, f, row, 6] = jnp.where(low_half, roll_s(q[par, u, f, row, 2], -1), roll_s(high, 1))
+                near_low, near_high = recv_c[par, u, low, f // 2], recv_c[par, u, high, f // 2]
+                if f % 2:
+                    near_low = roll_s(near_low, -1)
+                else:
+                    near_high = roll_s(near_high, 1)
+                q[par, u, f, row, 1] = jnp.where(low_half, near_low, roll_s(q[par, u, f, row, 5], 1))
+                q[par, u, f, row, 6] = jnp.where(low_half, roll_s(q[par, u, f, row, 2], -1), near_high)
 
     def sent_halos(par, u):
         for part in ("corner", "inner", "outer"):
@@ -239,6 +248,26 @@
         ]
         return center, rates
 
+    def fringe_copy(s, chunk):
+        part = fringe.at[s, pl.ds(*((1, 3), (4, 3), (0, 1), (7, 1))[chunk])]
+        return pltpu.make_async_remote_copy(
+            src_ref=part, dst_ref=part, send_sem=fs.at[s, chunk], recv_sem=fr.at[s, chunk],
+            device_id={"case": lax.rem(case + 1, n_case)}, device_id_type=MESH,
+        )
+
+    def pack_fringe(nxt, s, start, stop, step, chunks):
+        @pl.loop(start, stop, step=step)
+        def _(y):
+            for f in range(4):
+                parts = [q[nxt, 0, f, y + 2, 2 + k] for k in range(4)]
+                parts = [parts[0]] + [roll_s(parts[k], 2 * k) for k in (1, 2, 3)]
+                fringe[s, y, f] = jnp.where(
+                    sub < 4, jnp.where(sub < 2, parts[0], parts[1]), jnp.where(sub < 6, parts[2], parts[3])
+                )
+
+        for chunk in chunks:
+            fringe_copy(s, chunk).start()
+
     def advance(par, nxt, u, s):
         cos, sin = angle_cos[u], angle_sin[u]
         field = q.at[par, u]
@@ -288,13 +317,17 @@
                 for f in range(4):
                     q[nxt, u, f, row, z] = 0.5 * (field[f, row, z] + center[f]) + (0.5 * TIME_STEP) * rates[f]
 
-        pl.when(s > 0)(lambda: sent_halos(1 - par, u))
+        pl.when((s > 0) & ((u == 1) | (s != 1)))(lambda: sent_halos(1 - par, u))
 
         @pl.loop(3, 9, step=2)
         def _(row):
             second(row, range(2, 6))
             second(row + 1, range(2, 6))
 
+        @pl.when((case == 0) & (u == 0))
+        def _():
+            pack_fringe(nxt, s, 1, 7, 1, (0, 1))
+
         second(2, (3, 4))
         second(9, (3, 4))
 
@@ -311,29 +344,11 @@
         @pl.loop(0, 8)
         def _(y):
             for f in range(4):
-                packed = fringe[s, f, y]
+                packed = fringe[s, y, f]
                 for k in range(4):
                     value = q[nxt, u, f, y + 2, 2 + k]
                     q[nxt, u, f, y + 2, 2 + k] = value + ramp * (roll_s(packed, -2 * k) - value)
 
-    def fringe_copy(s, f, k=1):
-        return pltpu.make_async_remote_copy(
-            src_ref=fringe.at[s, f], dst_ref=fringe.at[s, f], send_sem=fs.at[s, f, k], recv_sem=fr.at[s, f],
-            device_id={"case": lax.rem(case + k, n_case)}, device_id_type=MESH,
-        )
-
-    def pack_fringe(nxt, s):
-        for f in range(4):
-            @pl.loop(0, 8)
-            def _(y):
-                parts = [roll_s(q[nxt, 0, f, y + 2, 2 + k], 2 * k) if k else q[nxt, 0, f, y + 2, 2] for k in range(4)]
-                fringe[s, f, y] = jnp.where(
-                    sub < 4, jnp.where(sub < 2, parts[0], parts[1]), jnp.where(sub < 6, parts[2], parts[3])
-                )
-
-            fringe_copy(s, f, 2).start()
-            fringe_copy(s, f, 1).start()
-
     def emit(nxt, u):
         @pl.loop(0, 8)
         def _(y):
@@ -352,55 +367,51 @@
 
         if u == 0:
             pl.semaphore_wait(barrier, len(partners))
+        if u == 1:
+            sent_halos(0, 0)
         send_halos(0, u)
 
     constants()
 
-    @pl.loop(0, STEPS)
-    def _(s):
+    ahead = ((0, 0), (1, 0), (0, 1), (1, 1), (0, 2), (1, 2))
+
+    @pl.loop(0, 2 * STEPS)
+    def _(task):
+        u, s = lax.rem(task, 2), lax.div(task, 2)
+        for spot, (slot, step) in enumerate(ahead):
+            here = (case == 0) & (task == spot)
+            u, s = jnp.where(here, slot, u), jnp.where(here, step, s)
         par = lax.rem(s, 2)
         nxt = 1 - par
         more = s < STEPS - 1
-        advance(par, nxt, 0, s)
-
-        @pl.when(case == 0)
-        def _():
-            pack_fringe(nxt, s)
-
-        @pl.when((case == 0) & more)
+        first_slot = u == 0
+        early = ((s > 0) | (case == 1)) & ((s < STEPS - 1) | (case < n_case - 1))
+
+        advance(par, nxt, u, s)
+
+        @pl.when((case == 0) & first_slot)
+        def _():
+            pack_fringe(nxt, s, 0, 8, 7, (2, 3))
+
+        @pl.when((case > 0) & (first_slot == early))
+        def _():
+            for f in range(4):
+                fringe_copy(s, f).wait_recv()
+                pl.when(case < n_case - 1)(fringe_copy(s, f).start)
+            blend(nxt, 0, s)
+
+        @pl.when(more & ((case == 0) & first_slot | (case > 0) & (first_slot == early)))
         def _():
             send_halos(nxt, 0)
 
-        def finish_first():
-            for f in range(4):
-                fringe_copy(s, f).wait_recv()
-                pl.when(case == 2)(fringe_copy(s, f).start)
-            blend(nxt, 0, s)
-
-            @pl.when(more)
-            def _():
-                send_halos(nxt, 0)
-
-        pl.when((case > 0) & (s > 0))(finish_first)
-
-        advance(par, nxt, 1, s)
-
-        pl.when((case > 0) & (s == 0))(finish_first)
-
-        blend(nxt, 1, s)
-
-        @pl.when(more)
-        def _():
-            send_halos(nxt, 1)
-
-        @pl.when(case == 0)
-        def _():
-            for f in range(4):
-                for k in (1, 2):
-                    fringe_copy(s, f, k).wait_send()
-
-        @pl.when(case == 2)
-        def _():
+        @pl.when(jnp.logical_not(first_slot))
+        def _():
+            blend(nxt, 1, s)
+            pl.when(more)(lambda: send_halos(nxt, 1))
+
+    @pl.when(case < n_case - 1)
+    def _():
+        for s in range(STEPS):
             for f in range(4):
                 fringe_copy(s, f).wait_send()
 
@@ -427,8 +438,9 @@
             pltpu.VMEM(domain[1:], jnp.float32),
             pltpu.VMEM((2, 2, 2, 2, 4, 4, 8, 128), jnp.float32),
             pltpu.VMEM((2, 2, 2, 2, 4, 4, 8, 128), jnp.float32),
-            pltpu.VMEM((2, 2, 4, 4, 8, 128), jnp.float32),
-            pltpu.VMEM((STEPS, 4, 8, 8, 128), jnp.float32),
+            pltpu.VMEM((2, 2, 4, 2, 8, 128), jnp.float32),
+            pltpu.VMEM((2, 2, 4, 2, 8, 128), jnp.float32),
+            pltpu.VMEM((STEPS, 8, 4, 8, 128), jnp.float32),
             pltpu.VMEM((2, 3, 12, 8, 128), jnp.float32),
             pltpu.VMEM((2, 8, 128), jnp.float32),
             pltpu.VMEM((2, 8, 128), jnp.float32),
@@ -439,7 +451,7 @@
             pltpu.SemaphoreType.DMA((5,)),
             pltpu.SemaphoreType.DMA((2, 2, 12)),
             pltpu.SemaphoreType.DMA((2, 2, 12)),
-            pltpu.SemaphoreType.DMA((STEPS, 4, 4)),
+            pltpu.SemaphoreType.DMA((STEPS, 4)),
             pltpu.SemaphoreType.DMA((STEPS, 4)),
         ],
         compiler_params=pltpu.CompilerParams(

time: 62 us -> 57.9 us (0.934)
  Pallas kernels: 59.2 us -> 55.5 us
    pallas_call x1, Pallas kernels: 59.2 us -> 55.5 us  [body(): pl.pallas_call(kernel, out_shape=jax.ShapeDtypeStruct(tiled.shape, jnp.fl...]
where the time goes in v2:
time: 57.9 us; the launch traced here: 57.8 us
  Pallas kernels  55.5 us (96%)
  local copies, waits for them, and re-layouts  2.26 us (4%)
    pallas_call x1, Pallas kernels, body(): pl.pallas_call(kernel, out_shape=jax.ShapeDtypeStruct(tiled.shape, jnp.fl...  55.5 us
    unnamed x1, local copies, waits for them, and re-layouts  2.26 us

profile of v2, /device:TPU:96, one launch (start us, length us, event | category | flops | bytes accessed | tf_op | source)
XLA Modules:
  0.0 57.8 jit_solution(4531350153863296287)
XLA Ops:
  0.0 55.5 %heun_steps.1 = f32[2,4,8,32,128]{4,3,2,1,0:T(8,128)} custom-call(f32[2,4,8,32,128]{4,3,2,1,0:T(8,128)} %bitcast.11, s32[2,6]{1,0:T(2,128)} %tx_hbm.1, s32[2,6]{1,0:T(2,128)} %ty_hbm.1, s32[2]{0:T(128)} %yaw_hbm.1), custom_call_target="tpu_custom_call" | custom-call | tf_op jit(solution)/shard_map/heun_steps/pallas_call | solution.py:430
  55.6 2.3 %copy.6 = f32[2,4,8,8,512]{4,3,2,1,0:T(8,128)} copy(f32[2,4,8,8,512]{4,3,2,1,0:T(8,128)} %bitcast.10) | data formatting | bytes 2097152

commit v3 on v2

--- a/solution.py
+++ b/solution.py
@@ -42,19 +42,16 @@
         pltpu.make_async_copy(src, dst, load_sem.at[2 + i])
         for i, (src, dst) in enumerate(((tx_hbm, tx_ref), (ty_hbm, ty_ref), (yaw_hbm, yaw_ref)))
     ]
-    for copy in loads:
-        copy.start()
-
     barrier = pltpu.get_barrier_semaphore()
     partners = [
         {"span": s, "vert": v} for s in (left, span, right) for v in (below, vert, above)
     ]
     partners.pop(4)
-    partners += [
-        {"case": lax.rem(case + k, n_case)} for k in range(1, 4)
-    ]
+    partners += [{"case": lax.rem(case + k, n_case)} for k in (1, n_case - 1)]
     for partner in partners:
         pl.semaphore_signal(barrier, inc=1, device_id=partner, device_id_type=MESH)
+    for copy in loads:
+        copy.start()
 
     sub = lax.broadcasted_iota(jnp.int32, (8, 128), 0)
     lane = lax.broadcasted_iota(jnp.int32, (8, 128), 1)
@@ -215,7 +212,7 @@
             for copy, sends, _ in halo_copies(par, u, part):
                 guarded(sends, copy.wait_send)
 
-    def tendency(ref, u, row, z, cos, sin):
+    def tendency(ref, u, row, z, cos, sin, scale):
         center, gx, gy, gz, laplace = [], [], [], [], []
         for f in range(4):
             c = ref[f, row, z]
@@ -230,17 +227,18 @@
             gz.append(upper - lower)
             laplace.append(((east + west) + (north + south)) + (upper + lower) - 6.0 * c)
         strain = gx[1] * gx[1] + gy[2] * gy[2] + gz[3] * gz[3] + gy[1] * gy[1] + gz[1] * gz[1]
-        viscous = (0.5 * VISC) * jnp.sqrt(4.0 + strain)
+        viscous = (0.5 * scale * VISC) * jnp.sqrt(4.0 + strain)
         speed = 1.0 + center[1]
-        half_u, half_v, half_w = 0.5 * speed, 0.5 * center[2], 0.5 * center[3]
+        half = 0.5 * scale
+        half_u, half_v, half_w = half * speed, half * center[2], half * center[3]
         normal = speed * cos + center[2] * sin
         kind = 0 if z == 1 else 2 if z == 6 else 1
-        thrust = normal * jnp.abs(normal) * weight[u, kind, row]
+        thrust = normal * jnp.abs(normal) * (scale * weight[u, kind, row])
         extra = [
-            0.5 * (gx[1] + gy[2] + gz[3]),
-            0.5 * gx[0] + thrust * cos,
-            0.5 * gy[0] + thrust * sin,
-            0.5 * gz[0],
+            half * (gx[1] + gy[2] + gz[3]),
+            half * gx[0] + thrust * cos,
+            half * gy[0] + thrust * sin,
+            half * gz[0],
         ]
         rates = [
             viscous * laplace[f] - (half_u * gx[f] + half_v * gy[f] + half_w * gz[f] + extra[f])
@@ -274,9 +272,9 @@
 
         def first(row, zs):
             for z in zs:
-                center, rates = tendency(field, u, row, z, cos, sin)
+                center, rates = tendency(field, u, row, z, cos, sin, TIME_STEP)
                 for f in range(4):
-                    value = center[f] + TIME_STEP * rates[f]
+                    value = center[f] + rates[f]
                     if z == 1:
                         value = jnp.where(low_half & edge_low, 0.0, value)
                     if z == 6:
@@ -286,43 +284,35 @@
         edge_low = jnp.full((8, 128), vert, jnp.int32) == 0
         edge_high = jnp.full((8, 128), vert, jnp.int32) == n_vert - 1
 
-        @pl.loop(3, 9, step=3)
-        def _(row):
-            for r in range(3):
-                first(row + r, (3, 4))
+        for row in range(3, 9):
+            first(row, (3, 4))
 
         receive_inner(par, u)
 
         first(2, range(2, 6))
         first(9, range(2, 6))
 
-        @pl.loop(3, 9, step=3)
-        def _(row):
-            for r in range(3):
-                first(row + r, (2, 5))
+        for row in range(3, 9):
+            first(row, (2, 5))
 
         receive_outer(par, u)
 
         first(1, (3, 4))
         first(10, (3, 4))
 
-        @pl.loop(3, 9, step=3)
-        def _(row):
-            for r in range(3):
-                first(row + r, (1, 6))
+        for row in range(3, 9):
+            first(row, (1, 6))
 
         def second(row, zs):
             for z in zs:
-                center, rates = tendency(mid, u, row, z, cos, sin)
+                center, rates = tendency(mid, u, row, z, cos, sin, 0.5 * TIME_STEP)
                 for f in range(4):
-                    q[nxt, u, f, row, z] = 0.5 * (field[f, row, z] + center[f]) + (0.5 * TIME_STEP) * rates[f]
+                    q[nxt, u, f, row, z] = 0.5 * (field[f, row, z] + center[f]) + rates[f]
 
         pl.when((s > 0) & ((u == 1) | (s != 1)))(lambda: sent_halos(1 - par, u))
 
-        @pl.loop(3, 9, step=2)
-        def _(row):
+        for row in range(3, 9):
             second(row, range(2, 6))
-            second(row + 1, range(2, 6))
 
         @pl.when((case == 0) & (u == 0))
         def _():
@@ -349,12 +339,23 @@
                     value = q[nxt, u, f, y + 2, 2 + k]
                     q[nxt, u, f, y + 2, 2 + k] = value + ramp * (roll_s(packed, -2 * k) - value)
 
-    def emit(nxt, u):
+    def copy_out(u):
+        return pltpu.make_async_copy(stage.at[u], out_ref.at[u], load_sem.at[u])
+
+    def emit(nxt, u, blended):
+        ramp = ramp_ref[...]
+
         @pl.loop(0, 8)
         def _(y):
             for f in range(4):
+                packed = fringe[STEPS - 1, y, f]
                 for k in range(4):
-                    out_ref[u, f, y, pl.ds(k, 8, stride=4), :] = q[nxt, u, f, y + 2, 2 + k]
+                    value = q[nxt, u, f, y + 2, 2 + k]
+                    if blended:
+                        value = value + ramp * (roll_s(packed, -2 * k) - value)
+                    stage[u, f, y, pl.ds(k, 8, stride=4), :] = value
+
+        copy_out(u).start()
 
     for u in (0, 1):
         loads[u].wait()
@@ -373,14 +374,9 @@
 
     constants()
 
-    ahead = ((0, 0), (1, 0), (0, 1), (1, 1), (0, 2), (1, 2))
-
     @pl.loop(0, 2 * STEPS)
     def _(task):
         u, s = lax.rem(task, 2), lax.div(task, 2)
-        for spot, (slot, step) in enumerate(ahead):
-            here = (case == 0) & (task == spot)
-            u, s = jnp.where(here, slot, u), jnp.where(here, step, s)
         par = lax.rem(s, 2)
         nxt = 1 - par
         more = s < STEPS - 1
@@ -392,22 +388,28 @@
         @pl.when((case == 0) & first_slot)
         def _():
             pack_fringe(nxt, s, 0, 8, 7, (2, 3))
+            pl.when(jnp.logical_not(more))(lambda: emit(nxt, 0, False))
 
         @pl.when((case > 0) & (first_slot == early))
         def _():
-            for f in range(4):
-                fringe_copy(s, f).wait_recv()
-                pl.when(case < n_case - 1)(fringe_copy(s, f).start)
-            blend(nxt, 0, s)
+            for chunk in range(4):
+                fringe_copy(s, chunk).wait_recv()
+                pl.when(case < n_case - 1)(fringe_copy(s, chunk).start)
+            pl.when(more)(lambda: blend(nxt, 0, s))
+            pl.when(jnp.logical_not(more))(lambda: emit(nxt, 0, True))
 
         @pl.when(more & ((case == 0) & first_slot | (case > 0) & (first_slot == early)))
         def _():
             send_halos(nxt, 0)
 
-        @pl.when(jnp.logical_not(first_slot))
+        @pl.when(jnp.logical_not(first_slot) & more)
         def _():
             blend(nxt, 1, s)
-            pl.when(more)(lambda: send_halos(nxt, 1))
+            send_halos(nxt, 1)
+
+        @pl.when(jnp.logical_not(first_slot | more))
+        def _():
+            emit(nxt, 1, True)
 
     @pl.when(case < n_case - 1)
     def _():
@@ -416,9 +418,9 @@
                 fringe_copy(s, f).wait_send()
 
     for u in (0, 1):
-        emit(STEPS % 2, u)
+        sent_halos((STEPS - 1) % 2, u)
     for u in (0, 1):
-        sent_halos((STEPS - 1) % 2, u)
+        copy_out(u).wait()
 
 
 def body(state, turbine_x, turbine_y, yaw_index):
@@ -431,7 +433,7 @@
         kernel,
         out_shape=jax.ShapeDtypeStruct(tiled.shape, jnp.float32),
         in_specs=[pl.BlockSpec(memory_space=pltpu.HBM)] + [pl.BlockSpec(memory_space=pltpu.HBM)] * 3,
-        out_specs=pl.BlockSpec(memory_space=pltpu.VMEM),
+        out_specs=pl.BlockSpec(memory_space=pltpu.HBM),
         scratch_shapes=[
             pltpu.VMEM(tiled.shape, jnp.float32),
             pltpu.VMEM((2,) + domain, jnp.float32),

time: 57.9 us -> 56.7 us (0.979)
  Pallas kernels: 55.5 us -> 54.3 us
    pallas_call x1, Pallas kernels: 55.5 us -> 54.3 us  [body(): pl.pallas_call(kernel, out_shape=jax.ShapeDtypeStruct(tiled.shape, jnp.fl...]
where the time goes in v3:
time: 56.7 us; the launch traced here: 56.6 us
  Pallas kernels  54.3 us (96%)
  local copies, waits for them, and re-layouts  2.26 us (4%)
    pallas_call x1, Pallas kernels, body(): pl.pallas_call(kernel, out_shape=jax.ShapeDtypeStruct(tiled.shape, jnp.fl...  54.3 us
    unnamed x1, local copies, waits for them, and re-layouts  2.26 us

profile of v3, /device:TPU:96, one launch (start us, length us, event | category | flops | bytes accessed | tf_op | source)
XLA Modules:
  0.0 56.6 jit_solution(18091804499288221813)
XLA Ops:
  0.0 54.3 %heun_steps.1 = f32[2,4,8,32,128]{4,3,2,1,0:T(8,128)} custom-call(f32[2,4,8,32,128]{4,3,2,1,0:T(8,128)} %bitcast.11, s32[2,6]{1,0:T(2,128)} %tx_hbm.1, s32[2,6]{1,0:T(2,128)} %ty_hbm.1, s32[2]{0:T(128)} %yaw_hbm.1), custom_call_target="tpu_custom_call" | custom-call | tf_op jit(solution)/shard_map/heun_steps/pallas_call | solution.py:432
  54.3 2.3 %copy.6 = f32[2,4,8,8,512]{4,3,2,1,0:T(8,128)} copy(f32[2,4,8,8,512]{4,3,2,1,0:T(8,128)} %bitcast.10) | data formatting | bytes 2097152

commit v4 on v3

--- a/solution.py
+++ b/solution.py
@@ -160,6 +160,10 @@
         for copy, sends, _ in halo_copies(par, u, "corner"):
             guarded(sends, copy.start)
 
+        for part in ("inner", "outer"):
+            for copy, _, _ in halo_copies(par, u, part)[2:]:
+                copy.start()
+
         @pl.loop(0, 4)
         def _(y):
             for f in range(4):
@@ -170,8 +174,9 @@
                 send_z[par, u, 1, 0, f, y] = jnp.where(low_half, even[0], roll_s(odd[0], 1))
                 send_z[par, u, 1, 1, f, y] = jnp.where(low_half, even[1], roll_s(odd[1], 1))
 
-        for copy, sends, _ in halo_copies(par, u, "inner") + halo_copies(par, u, "outer"):
-            guarded(sends, copy.start)
+        for part in ("inner", "outer"):
+            for copy, sends, _ in halo_copies(par, u, part)[:2]:
+                guarded(sends, copy.start)
 
     def merge_z(par, u, layer):
         @pl.loop(0, 4)
@@ -311,12 +316,13 @@
 
         pl.when((s > 0) & ((u == 1) | (s != 1)))(lambda: sent_halos(1 - par, u))
 
-        for row in range(3, 9):
-            second(row, range(2, 6))
-
-        @pl.when((case == 0) & (u == 0))
-        def _():
-            pack_fringe(nxt, s, 1, 7, 1, (0, 1))
+        for start, chunk in ((3, 0), (6, 1)):
+            for row in range(start, start + 3):
+                second(row, range(2, 6))
+
+            @pl.when((case == 0) & (u == 0))
+            def _():
+                pack_fringe(nxt, s, start - 2, start + 1, 1, (chunk,))
 
         second(2, (3, 4))
         second(9, (3, 4))
@@ -328,10 +334,10 @@
         for row, z in ((2, 2), (2, 5), (9, 2), (9, 5)):
             second(row, (z,))
 
-    def blend(nxt, u, s):
+    def blend(nxt, u, s, start=0, stop=8):
         ramp = ramp_ref[...]
 
-        @pl.loop(0, 8)
+        @pl.loop(start, stop)
         def _(y):
             for f in range(4):
                 packed = fringe[s, y, f]
@@ -381,7 +387,7 @@
         nxt = 1 - par
         more = s < STEPS - 1
         first_slot = u == 0
-        early = ((s > 0) | (case == 1)) & ((s < STEPS - 1) | (case < n_case - 1))
+        early = ((s > 0) | (case < 3)) & ((s < STEPS - 1) | (case < n_case - 1))
 
         advance(par, nxt, u, s)
 
@@ -392,11 +398,14 @@
 
         @pl.when((case > 0) & (first_slot == early))
         def _():
-            for chunk in range(4):
+            for chunk, (start, stop) in enumerate(((1, 4), (4, 7), (0, 1), (7, 8))):
                 fringe_copy(s, chunk).wait_recv()
                 pl.when(case < n_case - 1)(fringe_copy(s, chunk).start)
-            pl.when(more)(lambda: blend(nxt, 0, s))
-            pl.when(jnp.logical_not(more))(lambda: emit(nxt, 0, True))
+                if chunk < 2:
+                    blend(nxt, 0, s, start, stop)
+            blend(nxt, 0, s, 0, 1)
+            blend(nxt, 0, s, 7, 8)
+            pl.when(jnp.logical_not(more))(lambda: emit(nxt, 0, False))
 
         @pl.when(more & ((case == 0) & first_slot | (case > 0) & (first_slot == early)))
         def _():

time: 56.7 us -> 56.5 us (level)
  no operation moved by 1% of the time
where the time goes in v4:
time: 56.5 us; the launch traced here: 56.3 us
  Pallas kernels  54.1 us (96%)
  local copies, waits for them, and re-layouts  2.26 us (4%)
    pallas_call x1, Pallas kernels, body(): pl.pallas_call(kernel, out_shape=jax.ShapeDtypeStruct(tiled.shape, jnp.fl...  54.1 us
    unnamed x1, local copies, waits for them, and re-layouts  2.26 us

profile of v4, /device:TPU:96, one launch (start us, length us, event | category | flops | bytes accessed | tf_op | source)
XLA Modules:
  0.0 56.3 jit_solution(7730369425350710154)
XLA Ops:
  0.0 54.1 %heun_steps.1 = f32[2,4,8,32,128]{4,3,2,1,0:T(8,128)} custom-call(f32[2,4,8,32,128]{4,3,2,1,0:T(8,128)} %bitcast.11, s32[2,6]{1,0:T(2,128)} %tx_hbm.1, s32[2,6]{1,0:T(2,128)} %ty_hbm.1, s32[2]{0:T(128)} %yaw_hbm.1), custom_call_target="tpu_custom_call" | custom-call | tf_op jit(solution)/shard_map/heun_steps/pallas_call | solution.py:441
  54.1 2.3 %copy.6 = f32[2,4,8,8,512]{4,3,2,1,0:T(8,128)} copy(f32[2,4,8,8,512]{4,3,2,1,0:T(8,128)} %bitcast.10) | data formatting | bytes 2097152
